TPU v7x, 512 devices: a whole 4x4x16 slice. The times are simulated.
512 devices in a mesh: dir: 8 (over x, core), texel: 64 (over z, y).
Axes of the slice: x: 4, y: 4, z: 16, core: 2. Of those that a mesh axis runs over, the one named last changes fastest.
Arguments:
- texels: bfloat16 [4096, 50176], P('texel', 'dir'), may hold values from -6 to 6
- labels: int32 [4096, 1], P('texel'), may hold values from 0 to 127; in each aligned block of 64 rows (0 to 63, 64 to 127, ...) at most 2 rows name the same one
- start_basis: bfloat16 [64, 50176], P(None, 'dir'), may hold values from -0.02734375 to 0.02734375
Outputs:
- coefficients: float32 [4096, 64], P('texel')
- bases: bfloat16 [128, 64, 50176], P('texel', None, 'dir')
Inputs may be any that keep to these rules, and one draw needn't show every extreme that they name: `labels`: among the rows of one index of texel (an aligned block of 64 rows) no cluster is named by more than 2 rows, a bound that some block reaches in every draw.
All inputs are finite; a program needn't handle non-finite values.
Results may differ from a plain program's by a relative error of at most 0.012.
Values may be sent and summed in bfloat16 or wider, within the bound.
A program may use at most 64 MiB of HBM per device.

v0:
```python
import jax
import jax.numpy as jnp
from jax import lax
from jax.sharding import PartitionSpec as P

COLS = 50176
K = 64
CL_DEV = 2
ITERS = 2


ridge_share = 0.05


def per_device(texels, labels, start_basis):
    row_count = texels.shape[0]
    col_width = texels.shape[1]
    groups = lax.axis_size("texel")
    slot_cap = max(2, 2 * row_count // (CL_DEV * groups))
    label_col = labels[:, 0]
    owners = label_col // CL_DEV
    local_idx = label_col % CL_DEV
    row_ids = jnp.arange(row_count, dtype=jnp.int32)
    matches = (label_col[None, :] == label_col[:, None]) & (row_ids[None, :] < row_ids[:, None])
    slot_rank = jnp.sum(matches.astype(jnp.int32), axis=1)
    slot_of_row = local_idx * (groups * slot_cap) + owners * slot_cap + slot_rank
    total_slots = CL_DEV * groups * slot_cap
    slot_ids = jnp.arange(total_slots, dtype=jnp.int32)
    slot_hit = slot_of_row[None, :] == slot_ids[:, None]
    source_row = jnp.sum(jnp.where(slot_hit, row_ids[None, :], 0), axis=1)
    filled = jnp.any(slot_hit, axis=1)
    outgoing = jnp.where(
        filled[:, None], jnp.take(texels, source_row, axis=0), jnp.zeros((), texels.dtype)
    )
    outgoing = outgoing.reshape(CL_DEV, groups * slot_cap, col_width)
    received = lax.all_to_all(outgoing, "texel", split_axis=1, concat_axis=1, tiled=True)
    ridge_term = jnp.float32(ridge_share * COLS)
    identity = jnp.broadcast_to(jnp.eye(K, dtype=jnp.float32), (CL_DEV, K, K))
    basis_now = jnp.broadcast_to(start_basis, (CL_DEV, K, col_width))
    highest = lax.Precision.HIGHEST
    for sweep in range(ITERS):
        local_proj = jnp.einsum(
            "crw,ckw->crk", received, basis_now, preferred_element_type=jnp.float32
        )
        summed_proj = lax.psum(local_proj, "dir")
        projected = summed_proj.astype(jnp.bfloat16)
        widened = jnp.einsum(
            "crk,crw->ckw", projected, received, preferred_element_type=jnp.float32
        ) + ridge_term * basis_now.astype(jnp.float32)
        gram_mat = lax.psum(
            jnp.einsum(
                "ckw,clw->ckl",
                widened,
                widened,
                precision=highest,
                preferred_element_type=jnp.float32,
            ),
            "dir",
        )
        lower_tri = jnp.linalg.cholesky(gram_mat)
        inverse = jax.scipy.linalg.solve_triangular(lower_tri, identity, lower=True)
        basis_now = jnp.einsum(
            "ckl,clw->ckw", inverse, widened, precision=highest, preferred_element_type=jnp.float32
        ).astype(jnp.bfloat16)
    partial_value = jnp.einsum(
        "crw,ckw->crk", received, basis_now, preferred_element_type=jnp.float32
    )
    summed = lax.psum(partial_value.astype(jnp.bfloat16), "dir").astype(jnp.float32)
    returned = lax.all_to_all(
        summed.astype(jnp.bfloat16), "texel", split_axis=1, concat_axis=1, tiled=True
    ).astype(summed.dtype)
    coefficients = returned.reshape(total_slots, K)[slot_of_row]
    return (coefficients, basis_now)


def solution(mesh):
    in_specs = (P("texel", "dir"), P("texel", None), P(None, "dir"))
    out_specs = (P("texel", None), P("texel", None, "dir"))
    return jax.shard_map(
        per_device, mesh=mesh, in_specs=in_specs, out_specs=out_specs, check_vma=False
    )
```

profile of v0, /device:TPU:8, one launch (start us, length us, event | category | flops | bytes accessed | tf_op | source)
XLA Modules:
  0.0 404.1 jit_solution(9749141329993377410)
XLA Ops:
  0.6 0.0 copy-start
  0.6 0.9 convert_reduce_fusion
  1.6 0.7 fusion.27
  2.2 0.1 select_reduce_fusion.2
  2.3 0.1 fusion.18
  2.5 0.1 copy.65
  2.6 0.1 copy.64
  2.8 4.2 %gather_fusion = bf16[256,6272]{1,0:T(8,128)(2,1)} fusion(bf16[64,6272]{1,0:T(8,128)(2,1)S(1)} %copy-done, s32[1024]{0:T(1024)S(1)} %pad_clamp_fusion.1), kind=kCustom, calls=%fused_computation | custom fusion | bytes 6423552 | tf_op jit(solution)/shard_map/jit(_take)/gather | solution.py:33
  7.0 8.2 %broadcast_select_fusion.1 = bf16[2,128,6272]{2,0,1:T(2,128)(2,1)} fusion(pred[2,128]{0,1:T(8,128)(4,1)S(1)} %copy.64, pred[2,128]{0,1:T(8,128)(4,1)S(1)} %copy.65, bf16[2,128,6272]{2,1,0:T(8,128)(2,1)} %bitcast.47), kind=kLoop, calls=%fused_computation.7 | loop fusion | flops 3211264 | bytes 6423040 | tf_op jit(solution)/shard_map/jit(_where)/select_n | solution.py:32
  15.2 19.0 %all-to-all-start = ((bf16[2,128,6272]{2,0,1:T(2,128)(2,1)}), bf16[2,128,6272]{2,0,1:T(2,128)(2,1)}, u32[]{:S(2)}, u32[]{:S(2)}) async-start(bf16[2,128,6272]{2,0,1:T(2,128)(2,1)} %broadcast_select_fusion.1), calls=%async_computation | async-start | bytes 6422528 | tf_op jit(solution)/shard_map/all_to_all | solution.py:36
  34.2 0.1 convert_multiply_fusion
  34.4 147.6 %all-to-all-done = bf16[2,128,6272]{2,0,1:T(2,128)(2,1)} async-done(((bf16[2,128,6272]{2,0,1:T(2,128)(2,1)}), bf16[2,128,6272]{2,0,1:T(2,128)(2,1)}, u32[]{:S(2)}, u32[]{:S(2)}) %all-to-all-start) | async-done | bytes 3211296 | tf_op jit(solution)/shard_map/all_to_all | solution.py:36
  182.0 3.1 fusion.2
  185.1 24.1 %psum.35 = bf16[2,128,64]{1,2,0:T(8,128)(2,1)S(1)} all-reduce(f32[2,128,64]{1,2,0:T(8,128)S(1)} %fusion.2), channel_id=1, replica_groups=mesh['dir'=8,'texel'=64] {'dir'}, use_global_device_ids=true, to_apply=%region_3.4 | all-reduce | flops 16384 | bytes 98304 | tf_op jit(solution)/shard_map/psum | solution.py:45
  209.3 2.7 convolution_add_fusion.1
  212.0 1.7 copy-done.2
  213.7 3.1 fusion.32
  216.8 23.9 %psum.36 = f32[2,64,64]{1,2,0:T(8,128)S(1)} all-reduce(f32[2,64,64]{1,2,0:T(8,128)S(1)} %fusion.32), channel_id=1, replica_groups=mesh['dir'=8,'texel'=64] {'dir'}, use_global_device_ids=true, to_apply=%region_4.5 | all-reduce | flops 8192 | bytes 65536 | tf_op jit(solution)/shard_map/psum | solution.py:50
  240.8 0.1 copy.70
  240.9 11.7 %custom-call.8 = f32[2,64,64]{2,1,0:T(8,128)S(1)} custom-call(f32[2,64,64]{2,1,0:T(8,128)S(1)} %fusion.17), custom_call_target="Cholesky" | custom-call | tf_op jit(solution)/shard_map/jit(cholesky)/cholesky | solution.py:60
  252.7 0.1 compare_reduce_fusion.1
  252.8 0.1 select_bitcast_fusion.1
  252.9 9.8 %custom-call.9 = f32[2,1,64,64]{2,3,1,0:T(8,128)S(1)} custom-call(f32[2,1,64,64]{3,2,1,0:T(8,128)S(1)} %select_bitcast_fusion.1), custom_call_target="InvertDiagBlocksLowerTriangular" | custom-call | tf_op jit(solution)/shard_map/jit(_solve_triangular)/vmap()/triangular_solve | solution.py:61
  262.7 0.3 fusion.15
  263.0 4.7 %convolution_convert_fusion.1 = bf16[2,64,6272]{2,1,0:T(8,128)(2,1)S(1)} fusion(f32[2,64,64]{2,1,0:T(8,128)S(1)} %fusion.15, f32[2,64,6272]{2,1,0:T(8,128)} %copy-done.2), kind=kOutput, calls=%fused_computation.5 | convolution fusion | flops 617365504 | bytes 4849664 | tf_op jit(solution)/shard_map/ckl,clw->ckw/dot_general | solution.py:62
  267.7 3.1 fusion.4
  270.9 24.2 %psum.37 = bf16[2,128,64]{1,2,0:T(8,128)(2,1)S(1)} all-reduce(f32[2,128,64]{1,2,0:T(8,128)S(1)} %fusion.4), channel_id=1, replica_groups=mesh['dir'=8,'texel'=64] {'dir'}, use_global_device_ids=true, to_apply=%region_7.10 | all-reduce | flops 16384 | bytes 98304 | tf_op jit(solution)/shard_map/psum | solution.py:45
  295.1 2.6 convolution_add_fusion
  297.7 1.7 copy-done.1
  299.4 3.1 fusion.33
  302.5 23.9 %psum.38 = f32[2,64,64]{1,2,0:T(8,128)S(1)} all-reduce(f32[2,64,64]{1,2,0:T(8,128)S(1)} %fusion.33), channel_id=1, replica_groups=mesh['dir'=8,'texel'=64] {'dir'}, use_global_device_ids=true, to_apply=%region_8.11 | all-reduce | flops 8192 | bytes 65536 | tf_op jit(solution)/shard_map/psum | solution.py:50
  326.5 0.1 copy.75
  326.6 11.7 %custom-call.10 = f32[2,64,64]{2,1,0:T(8,128)S(1)} custom-call(f32[2,64,64]{2,1,0:T(8,128)S(1)} %fusion.14), custom_call_target="Cholesky" | custom-call | tf_op jit(solution)/shard_map/jit(cholesky)/cholesky | solution.py:60
  338.4 0.1 compare_reduce_fusion
  338.5 0.1 select_bitcast_fusion
  338.6 9.8 %custom-call.11 = f32[2,1,64,64]{2,3,1,0:T(8,128)S(1)} custom-call(f32[2,1,64,64]{3,2,1,0:T(8,128)S(1)} %select_bitcast_fusion), custom_call_target="InvertDiagBlocksLowerTriangular" | custom-call | tf_op jit(solution)/shard_map/jit(_solve_triangular)/vmap()/triangular_solve | solution.py:61
  348.4 0.3 fusion.12
  348.7 4.7 %convolution_convert_fusion = bf16[2,64,6272]{2,1,0:T(8,128)(2,1)S(1)} fusion(f32[2,64,64]{2,1,0:T(8,128)S(1)} %fusion.12, f32[2,64,6272]{2,1,0:T(8,128)} %copy-done.1), kind=kOutput, calls=%fused_computation.4 | convolution fusion | flops 617365504 | bytes 4849664 | tf_op jit(solution)/shard_map/ckl,clw->ckw/dot_general | solution.py:62
  353.5 3.7 fusion.8
  357.2 23.6 %psum.39 = bf16[2,128,64]{1,2,0:T(8,128)(2,1)S(1)} all-reduce(bf16[2,128,64]{1,2,0:T(8,128)(2,1)S(1)} %fusion.8), channel_id=1, replica_groups=mesh['dir'=8,'texel'=64] {'dir'}, use_global_device_ids=true, to_apply=%region_9.12 | all-reduce | flops 16384 | bytes 65536 | tf_op jit(solution)/shard_map/psum | solution.py:68
  380.8 0.1 copy.78
  381.0 0.7 reshape.126
  381.7 7.3 %all-to-all-start.1 = ((bf16[64,2,128]{2,1,0:T(2,128)(2,1)}), bf16[64,2,128]{2,1,0:T(2,128)(2,1)S(1)}, u32[]{:S(2)}, u32[]{:S(2)}) async-start(bf16[64,2,128]{2,1,0:T(2,128)(2,1)} %reshape.126), calls=%async_computation.1 | async-start | bytes 65536 | tf_op jit(solution)/shard_map/all_to_all | solution.py:69
  389.0 13.6 %all-to-all-done.1 = bf16[64,2,128]{2,1,0:T(2,128)(2,1)S(1)} async-done(((bf16[64,2,128]{2,1,0:T(2,128)(2,1)}), bf16[64,2,128]{2,1,0:T(2,128)(2,1)S(1)}, u32[]{:S(2)}, u32[]{:S(2)}) %all-to-all-start.1) | async-done | bytes 32800 | tf_op jit(solution)/shard_map/all_to_all | solution.py:69
  402.6 0.1 reshape.127
  402.7 0.1 copy.79
  402.8 0.1 copy.86
  402.9 1.2 gather_fusion.1
  (21 shorter events, 0.2 us)
Async XLA Ops:
  0.6 2.1 copy-start
  15.2 19.1 %copy-start.4 = (bf16[64,6272]{1,0:T(8,128)(2,1)S(1)}, bf16[64,6272]{1,0:T(8,128)(2,1)}, u32[]{:S(2)}) copy-start(bf16[64,6272]{1,0:T(8,128)(2,1)} %param.8) | copy-start | bytes 2408452
  15.2 166.8 %all-to-all-start = ((bf16[2,128,6272]{2,0,1:T(2,128)(2,1)}), bf16[2,128,6272]{2,0,1:T(2,128)(2,1)}, u32[]{:S(2)}, u32[]{:S(2)}) async-start(bf16[2,128,6272]{2,0,1:T(2,128)(2,1)} %broadcast_select_fusion.1), calls=%async_computation | async-start | bytes 6422528 | tf_op jit(solution)/shard_map/all_to_all | solution.py:36
  212.0 1.7 copy-start.2
  297.7 1.7 copy-start.1
  353.4 50.7 %copy-start.3 = (bf16[2,64,6272]{2,1,0:T(8,128)(2,1)}, bf16[2,64,6272]{2,1,0:T(8,128)(2,1)S(1)}, u32[]{:S(2)}) copy-start(bf16[2,64,6272]{2,1,0:T(8,128)(2,1)S(1)} %convolution_convert_fusion) | copy-start | bytes 4816900
  353.5 35.5 %copy-start.5 = (s32[64,1]{0,1:T(1,128)S(1)}, s32[64,1]{0,1:T(1,128)}, u32[]{:S(2)}) copy-start(s32[64,1]{0,1:T(1,128)} %param.7) | copy-start | bytes 772
  381.7 21.0 %all-to-all-start.1 = ((bf16[64,2,128]{2,1,0:T(2,128)(2,1)}), bf16[64,2,128]{2,1,0:T(2,128)(2,1)S(1)}, u32[]{:S(2)}, u32[]{:S(2)}) async-start(bf16[64,2,128]{2,1,0:T(2,128)(2,1)} %reshape.126), calls=%async_computation.1 | async-start | bytes 65536 | tf_op jit(solution)/shard_map/all_to_all | solution.py:69
where the time goes:
time: 405 us; the launch traced here: 404 us
  waiting for transfers between devices  161 us (40%)
  blocking collectives  120 us (30%)
  other arithmetic  53.8 us (13%)
  matrix products  31.7 us (8%)
  starting transfers between devices  26.3 us (6%)
  local copies, waits for them, and re-layouts  10.4 us (3%)
    all_to_all x1, waiting for transfers between devices, per_device(): lax.all_to_all(outgoing, 'texel', split_axis=1, concat_axis=1, tiled=True)  148 us
    psum x2, blocking collectives, per_device(): summed_proj = lax.psum(local_proj, 'dir')  48.3 us
    psum x2, blocking collectives, per_device(): lax.psum(jnp.einsum('ckw,clw->ckl', widened, widened, precision=highest,...  47.9 us
    another operation x7, other arithmetic, per_device(): lower_tri = jnp.linalg.cholesky(gram_mat)  23.8 us
    psum x1, blocking collectives, per_device(): lax.psum(partial_value.astype(jnp.bfloat16), 'dir').astype(jnp.float32)  23.6 us
    another operation x5, other arithmetic, per_device(): inverse = jax.scipy.linalg.solve_triangular(lower_tri, identity, lower=True)  19.8 us
    all_to_all x1, starting transfers between devices, per_device(): lax.all_to_all(outgoing, 'texel', split_axis=1, concat_axis=1, tiled=True)  19 us
    all_to_all x1, waiting for transfers between devices, per_device(): lax.all_to_all(summed.astype(jnp.bfloat16), 'texel', split_axis=1, concat...  13.6 us
  transfers between devices with their start and end apart: 2, of which 2 were waited for; matrix products, arithmetic and copies ran while one was open for 0% of the time, Pallas kernels for 0%

commit v1 on v0

v1 whole, which is shorter than its diff:
```python
import jax
import jax.numpy as jnp
from jax import lax
from jax.experimental import pallas as pl
from jax.experimental.pallas import tpu as pltpu
from jax.sharding import PartitionSpec as P

COLS = 50176
K = 64
CL_DEV = 2
ITERS = 2
RIDGE = 0.05 * COLS
HIGHEST = lax.Precision.HIGHEST


def mm(a, b):
    return jnp.dot(a, b, precision=HIGHEST, preferred_element_type=jnp.float32)


def mm_t(a, b):
    return lax.dot_general(
        a, b, (((1,), (1,)), ((), ())), precision=HIGHEST, preferred_element_type=jnp.float32
    )


def inverse_cholesky(grams):
    rows = lax.broadcasted_iota(jnp.int32, (K, 2 * K), 0)
    lanes = lax.broadcasted_iota(jnp.int32, (K, 2 * K), 1)
    eye = (lax.broadcasted_iota(jnp.int32, (K, K), 0) == lax.broadcasted_iota(jnp.int32, (K, K), 1)).astype(jnp.float32)
    work = [jnp.concatenate([g, eye], axis=1) for g in grams]
    for j in range(K - 1):
        for c in range(len(work)):
            a = work[c]
            row = a[j : j + 1, :]
            scaled = row * (1.0 / a[j : j + 1, j : j + 1])
            col = jnp.where(rows > j, jnp.broadcast_to(a[:, j : j + 1], (K, 2 * K)), 0.0)
            work[c] = a - col * scaled
    out = []
    for a in work:
        pivots = jnp.sum(jnp.where(rows == lanes, a, 0.0), axis=1, keepdims=True)
        out.append(a[:, K:] * (1.0 / jnp.sqrt(pivots)))
    return out


def update_kernel(gram_ref, rows_ref, start_ref, basis_ref, coef_ref):
    cl = range(CL_DEV)
    n = rows_ref.shape[1]
    base = CL_DEV * n
    g = [gram_ref[c * n : (c + 1) * n, :] for c in cl]
    pt = [gram_ref[base + c * K : base + (c + 1) * K, :] for c in cl]
    p = [jnp.transpose(pt[c]) for c in cl]
    s = gram_ref[base + CL_DEV * K :, :K]
    ridge = jnp.float32(RIDGE)
    gram1 = [
        mm_t(mm(pt[c], g[c]), pt[c]) + (2.0 * ridge) * mm_t(pt[c], pt[c]) + (ridge * ridge) * s
        for c in cl
    ]
    inv1 = inverse_cholesky(gram1)
    a1 = [mm(inv1[c], pt[c]) for c in cl]
    b1 = [ridge * inv1[c] for c in cl]
    p2t = [mm(a1[c], g[c]) + mm(b1[c], pt[c]) for c in cl]
    wa = [p2t[c] + ridge * a1[c] for c in cl]
    wb = [ridge * b1[c] for c in cl]
    yr = [mm(wa[c], g[c]) + mm(wb[c], pt[c]) for c in cl]
    ys = [mm(wa[c], p[c]) + mm(wb[c], s) for c in cl]
    gram2 = [mm_t(yr[c], wa[c]) + mm_t(ys[c], wb[c]) for c in cl]
    inv2 = inverse_cholesky(gram2)
    for c in cl:
        a2 = mm(inv2[c], wa[c])
        b2 = mm(inv2[c], wb[c])
        coef_ref[c] = jnp.transpose(mm(a2, g[c]) + mm(b2, pt[c])).astype(coef_ref.dtype)
        a_hi = a2.astype(jnp.bfloat16)
        a_lo = (a2 - a_hi.astype(jnp.float32)).astype(jnp.bfloat16)
        b_hi = b2.astype(jnp.bfloat16)
        b_lo = (b2 - b_hi.astype(jnp.float32)).astype(jnp.bfloat16)
        width = basis_ref.shape[2] // 7
        for w in range(7):
            cols = slice(w * width, (w + 1) * width)
            r = rows_ref[c, :, cols]
            b = start_ref[:, cols]
            f32 = jnp.float32
            acc = jnp.dot(a_hi, r, preferred_element_type=f32) + jnp.dot(a_lo, r, preferred_element_type=f32)
            acc += jnp.dot(b_hi, b, preferred_element_type=f32) + jnp.dot(b_lo, b, preferred_element_type=f32)
            basis_ref[c, :, cols] = acc.astype(basis_ref.dtype)


def update(gram, rows, start):
    c, r, w = rows.shape
    vmem = pl.BlockSpec(memory_space=pltpu.VMEM)
    return pl.pallas_call(
        update_kernel,
        name="update",
        out_shape=(
            jax.ShapeDtypeStruct((c, K, w), jnp.bfloat16),
            jax.ShapeDtypeStruct((c, r, K), jnp.bfloat16),
        ),
        in_specs=[vmem] * 3,
        out_specs=(vmem, vmem),
        compiler_params=pltpu.CompilerParams(vmem_limit_bytes=48 * 1024 * 1024),
    )(gram, rows, start)


def per_device(texels, labels, start_basis):
    row_count = texels.shape[0]
    col_width = texels.shape[1]
    groups = lax.axis_size("texel")
    slot_cap = max(2, 2 * row_count // (CL_DEV * groups))
    label_col = labels[:, 0]
    owners = label_col // CL_DEV
    local_idx = label_col % CL_DEV
    row_ids = jnp.arange(row_count, dtype=jnp.int32)
    matches = (label_col[None, :] == label_col[:, None]) & (row_ids[None, :] < row_ids[:, None])
    slot_rank = jnp.sum(matches.astype(jnp.int32), axis=1)
    slot_of_row = local_idx * (groups * slot_cap) + owners * slot_cap + slot_rank
    total_slots = CL_DEV * groups * slot_cap
    slot_ids = jnp.arange(total_slots, dtype=jnp.int32)
    slot_hit = slot_of_row[None, :] == slot_ids[:, None]
    pick = slot_hit.astype(jnp.bfloat16)
    outgoing = jnp.dot(pick, texels, preferred_element_type=jnp.float32).astype(jnp.bfloat16)
    outgoing = outgoing.reshape(CL_DEV, groups * slot_cap, col_width)
    received = lax.all_to_all(outgoing, "texel", split_axis=1, concat_axis=1, tiled=True)
    f32 = jnp.float32
    grr = jnp.einsum("crw,csw->crs", received, received, preferred_element_type=f32)
    gsr = jnp.einsum("kw,crw->ckr", start_basis, received, preferred_element_type=f32)
    gss = jnp.einsum("jw,kw->jk", start_basis, start_basis, preferred_element_type=f32)
    n = received.shape[1]
    parts = (grr.reshape(CL_DEV * n, n), gsr.reshape(CL_DEV * K, n), jnp.pad(gss, ((0, 0), (0, n - K))))
    gram = lax.psum(jnp.concatenate(parts, axis=0), "dir")
    basis, summed = update(gram, received, start_basis)
    returned = lax.all_to_all(summed, "texel", split_axis=1, concat_axis=1, tiled=True)
    returned = returned.reshape(total_slots, K)
    coefficients = jnp.dot(pick.T, returned, preferred_element_type=f32)
    return (coefficients, basis)


def solution(mesh):
    in_specs = (P("texel", "dir"), P("texel", None), P(None, "dir"))
    out_specs = (P("texel", None), P("texel", None, "dir"))
    return jax.shard_map(
        per_device, mesh=mesh, in_specs=in_specs, out_specs=out_specs, check_vma=False
    )
```

time: 405 us -> 313 us (0.77)
  blocking collectives: 120 us -> 29.4 us
  other arithmetic: 53.8 us -> 2.3 us
  waiting for transfers between devices: 161 us -> 209 us
  matrix products: 31.7 us -> 9 us
  Pallas kernels: 0 us -> 17.8 us
  between operations: 0.93 us -> 14.1 us
  starting transfers between devices: 26.3 us -> 19.2 us
    psum x5 -> x0, blocking collectives: 120 us -> none  [the longest x2 48.3 us: per_device(): summed_proj = lax.psum(local_proj, 'dir')]
    psum x0 -> x1, waiting for transfers between devices: none -> 61.9 us  [per_device(): gram = lax.psum(jnp.concatenate(parts, axis=0), 'dir')]
    another operation x12 -> x0, other arithmetic: 43.6 us -> none  [the longest x7 23.8 us: per_device(): lower_tri = jnp.linalg.cholesky(gram_mat)]
    all_to_all x0 -> x1, blocking collectives: none -> 29.4 us  [per_device(): lax.all_to_all(summed, 'texel', split_axis=1, concat_axis=1, tiled=True)]
    dot_general x9 -> x5, matrix products: 31.1 us -> 9 us  [the longest x1 3.9 us: per_device(): jnp.einsum('crw,csw->crs', received, received, preferred_element_type=f32)]
    pallas_call x0 -> x1, Pallas kernels: none -> 17.8 us  [update(): pl.pallas_call(update_kernel, name='update', out_shape=(jax.ShapeDtypeStr...]
    all_to_all x1 -> x0, waiting for transfers between devices: 13.6 us -> none  [per_device(): lax.all_to_all(summed.astype(jnp.bfloat16), 'texel', split_axis=1, concat...]
    select_n x3 -> x0, other arithmetic: 8.19 us -> none  [the longest x1 8.17 us: per_device(): jnp.where(filled[:, None], jnp.take(texels, source_row, axis=0), jnp.zero...]
  transfers between devices with their start and end apart: 2 -> 2, of which waited for: 2 -> 2; matrix products, arithmetic and copies ran while one was open for 0% -> 1% of each run, Pallas kernels for 0% -> 0%
where the time goes in v1:
time: 313 us
  waiting for transfers between devices  209 us (67%)
  blocking collectives  29.4 us (9%)
  starting transfers between devices  19.2 us (6%)
  Pallas kernels  17.8 us (6%)
  between operations  14.1 us (5%)
  local copies, waits for them, and re-layouts  12.1 us (4%)
  matrix products  9 us (3%)
    all_to_all x1, waiting for transfers between devices, per_device(): lax.all_to_all(outgoing, 'texel', split_axis=1, concat_axis=1, tiled=True)  147 us
    psum x1, waiting for transfers between devices, per_device(): gram = lax.psum(jnp.concatenate(parts, axis=0), 'dir')  61.9 us
    all_to_all x1, blocking collectives, per_device(): lax.all_to_all(summed, 'texel', split_axis=1, concat_axis=1, tiled=True)  29.4 us
    all_to_all x1, starting transfers between devices, per_device(): lax.all_to_all(outgoing, 'texel', split_axis=1, concat_axis=1, tiled=True)  19 us
    pallas_call x1, Pallas kernels, update(): pl.pallas_call(update_kernel, name='update', out_shape=(jax.ShapeDtypeStr...  17.8 us
  transfers between devices with their start and end apart: 2, of which 2 were waited for; matrix products, arithmetic and copies ran while one was open for 1% of the time, Pallas kernels for 0%

profile of v1, /device:TPU:8, one launch (start us, length us, event | category | flops | bytes accessed | tf_op | source)
XLA Modules:
  0.0 313.0 jit_solution(17412016914962624241)
XLA Ops:
  7.2 0.0 copy-start
  7.2 0.9 convert_reduce_fusion
  8.1 0.7 fusion.12
  8.8 0.0 copy-done
  8.8 1.0 convolution_convert_fusion
  9.8 5.0 %copy.18 = bf16[2,128,6272]{2,0,1:T(2,128)(2,1)} copy(bf16[2,128,6272]{2,1,0:T(8,128)(2,1)S(1)} %bitcast.23) | data formatting | bytes 6422528 | tf_op jit(solution)/shard_map/reshape | solution.py:120
  14.8 0.0 copy-start.2
  14.8 19.0 %all-to-all-start = ((bf16[2,128,6272]{2,0,1:T(2,128)(2,1)}), bf16[2,128,6272]{2,0,1:T(2,128)(2,1)}, u32[]{:S(2)}, u32[]{:S(2)}) async-start(bf16[2,128,6272]{2,0,1:T(2,128)(2,1)} %copy.18), calls=%async_computation | async-start | bytes 6422528 | tf_op jit(solution)/shard_map/all_to_all | solution.py:121
  33.8 0.2 all-reduce.3.cloned.1.call-start
  34.0 0.0 copy-done.2
  34.0 0.3 fusion.16
  34.4 147.2 %all-to-all-done = bf16[2,128,6272]{2,0,1:T(2,128)(2,1)} async-done(((bf16[2,128,6272]{2,0,1:T(2,128)(2,1)}), bf16[2,128,6272]{2,0,1:T(2,128)(2,1)}, u32[]{:S(2)}, u32[]{:S(2)}) %all-to-all-start) | async-done | bytes 3211296 | tf_op jit(solution)/shard_map/all_to_all | solution.py:121
  181.6 3.0 fusion
  184.6 3.9 %fusion.14 = f32[2,128,128]{2,1,0:T(8,128)S(1)} fusion(bf16[2,128,6272]{2,0,1:T(2,128)(2,1)} %all-to-all-done), kind=kOutput, calls=%fused_computation.24 | convolution fusion | flops 411041792 | bytes 3342336 | tf_op jit(solution)/shard_map/crw,csw->crs/dot_general | solution.py:123
  188.5 0.7 select_maximum_fusion
  189.2 0.0 all-reduce.3.cloned.1.call-update
  189.2 3.9 %copy.19.rows_ref = bf16[2,128,6272]{2,1,0:T(8,128)(2,1)} copy(bf16[2,128,6272]{2,0,1:T(2,128)(2,1)} %all-to-all-done) | data formatting | bytes 6422528 | tf_op jit(solution)/shard_map/all_to_all | solution.py:121
  193.1 61.9 %all-reduce.3.cloned.1.call-done.gram_ref = f32[448,128]{1,0:T(8,128)} async-done(((f32[448,128]{1,0:T(8,128)}), f32[448,128]{1,0:T(8,128)}) %all-reduce.3.cloned.1.call-update) | async-done | bytes 229392 | tf_op jit(solution)/shard_map/psum | solution.py:128
  255.0 0.0 copy-start.1
  255.0 1.9 copy-done.1
  256.9 0.0 copy-start.3
  256.9 0.9 copy-done.3
  257.9 17.8 %update.1 = (bf16[2,64,6272]{2,1,0:T(8,128)(2,1)}, bf16[2,128,64]{2,1,0:T(8,128)(2,1)S(1)}) custom-call(f32[448,128]{1,0:T(8,128)S(1)} %copy-done.3, bf16[2,128,6272]{2,1,0:T(8,128)(2,1)S(1)} %copy-done.1, bf16[64,6272]{1,0:T(8,128)(2,1)S(1)} %copy-done.2), custom_call_target="tpu_custom_call" | custom-call | tf_op jit(solution)/shard_map/update/pallas_call | solution.py:90
  275.6 0.1 copy.35
  275.7 0.1 reshape.76
  275.8 29.4 %all_to_all.10 = bf16[64,2,128]{2,1,0:T(2,128)(2,1)S(1)} all-to-all(bf16[64,2,128]{2,1,0:T(2,128)(2,1)S(1)} %reshape.76), channel_id=1, replica_groups=mesh['dir'=8,'texel'=64] {'texel'}, dimensions={0} | all-to-all | bytes 65536 | tf_op jit(solution)/shard_map/all_to_all | solution.py:130
  305.2 0.1 reshape.77
  305.3 0.1 copy.24
  305.4 0.8 fusion.3
Async XLA Ops:
  7.2 1.6 copy-start
  14.8 19.3 %copy-start.2 = (bf16[64,6272]{1,0:T(8,128)(2,1)S(1)}, bf16[64,6272]{1,0:T(8,128)(2,1)}, u32[]{:S(2)}) copy-start(bf16[64,6272]{1,0:T(8,128)(2,1)} %start_ref.1) | copy-start | bytes 2408452
  14.8 166.8 %all-to-all-start = ((bf16[2,128,6272]{2,0,1:T(2,128)(2,1)}), bf16[2,128,6272]{2,0,1:T(2,128)(2,1)}, u32[]{:S(2)}, u32[]{:S(2)}) async-start(bf16[2,128,6272]{2,0,1:T(2,128)(2,1)} %copy.18), calls=%async_computation | async-start | bytes 6422528 | tf_op jit(solution)/shard_map/all_to_all | solution.py:121
  33.8 221.2 %all-reduce.3.cloned.1.call-start = ((), (), s32[]{:S(2)}) async-start(), calls=%async_computation.2 | async-start | bytes 458752 | tf_op jit(solution)/shard_map/psum | solution.py:128
  255.0 1.9 copy-start.1
  256.9 0.9 copy-start.3
Sparse Core Ops, SparseCore 0:
  189.3 65.6 all-reduce.2
